TPU v7x, 32 devices: a whole 2x2x4 slice. The times are simulated.
32 devices in a mesh: groups: 2 (over y), ctx: 4 (over z), mp: 4 (over x, core).
Axes of the slice: x: 2, y: 2, z: 4, core: 2. Of those that a mesh axis runs over, the one named last changes fastest.
Arguments:
- query: bfloat16 [4096, 8192], P(('groups', 'ctx'), 'mp'), parts along dimension 0, may hold values from -200 to 200
- span_keys: bfloat16 [4096, 1024], P(('groups', 'ctx'), 'mp'), parts along dimension 0, may hold values from -6 to 6
- span_values: bfloat16 [4096, 1024], P(('groups', 'ctx'), 'mp'), parts along dimension 0, may hold values from -6 to 6
- cache_keys: bfloat16 [8192, 1024], P(('groups', 'ctx'), 'mp'), parts along dimension 0, may hold values from -13 to 13
- stored_values: bfloat16 [8192, 1024], P(('groups', 'ctx'), 'mp'), parts along dimension 0, may hold values from -6 to 6
- selected: int32 [8, 8, 2], P(('groups', 'ctx'), 'mp'), parts along dimension 0, may hold values from 0 to 7, as said below
Outputs:
- attended: bfloat16 [4096, 8192], P(('groups', 'ctx'), 'mp'), parts along dimension 0
There are 2 independent parts, one for each index of `groups`. A program takes and returns all parts, laid end to end along the dimension named above; each array names one. Nothing has to cross between parts.
Inputs may be any that keep to these rules, and one draw needn't show every extreme that they name: `selected`: the two blocks chosen for a query block and key head lie in different ranges of 2 consecutive blocks, starting at multiples of 2.
All inputs are finite; a program needn't handle non-finite values.
Results may differ from a plain program's by a relative error of at most 0.0047.
Values may be sent and summed in bfloat16 or wider, within the bound.
No kernel may reach another device: no remote copies, remote signals or barrier semaphores. Data moves between devices by JAX's collectives and lax.ppermute only.
A program may use at most 64 MiB of HBM per device.

v0:
```python
import jax
import jax.numpy as jnp
from jax import lax
from jax.experimental import pallas as pl
from jax.experimental.pallas import tpu as pltpu
from jax.sharding import PartitionSpec as P

HEAD = 128
LOG2E = 1.4426950408889634
NEG = -1e30
VMEM = pl.BlockSpec(memory_space=pltpu.VMEM)
ANY = pl.BlockSpec(memory_space=pl.ANY)
SMEM = pl.BlockSpec(memory_space=pltpu.SMEM)
PARAMS = pltpu.CompilerParams(vmem_limit_bytes=8 << 20)
WIDE = pltpu.CompilerParams(vmem_limit_bytes=20 << 20)


def near_core(x):
    return pltpu.with_memory_space_constraint(x, pltpu.VMEM)


def in_hbm(x):
    return pltpu.with_memory_space_constraint(x, pltpu.HBM)


def local_row(sel, owner, h, per_owner, at=0):
    a, b = sel[at, h, 0], sel[at, h, 1]
    lo = owner * per_owner
    in_a = (a >= lo) & (a < lo + per_owner)
    in_b = (b >= lo) & (b < lo + per_owner)
    return jnp.where(in_a, a - lo, jnp.where(in_b, b - lo, 0))


def wants(sel, owner, h, per_owner):
    a, b = sel[0, h, 0], sel[0, h, 1]
    lo = owner * per_owner
    return ((a >= lo) & (a < lo + per_owner)) | ((b >= lo) & (b < lo + per_owner))


def with_ones(v):
    return jnp.concatenate([v, jnp.ones((v.shape[0], HEAD), jnp.bfloat16)], axis=1)


def scores_of(q, k):
    return lax.dot_general(q, k, (((1,), (1,)), ((), ())), preferred_element_type=jnp.float32)


SCALE = LOG2E * HEAD ** -0.5


def own_rest(s, v, mask, first_key):
    s = jnp.concatenate([s[:, :first_key], s[:, first_key:] + mask], axis=1) if first_key else s + mask
    top = jnp.max(s, axis=1, keepdims=True)
    p = jnp.exp2((s - top) * SCALE).astype(jnp.bfloat16)
    sums = jnp.dot(p, v, preferred_element_type=jnp.float32)
    return sums[:, :HEAD], sums[:, HEAD:], jnp.broadcast_to(top, (s.shape[0], HEAD))


def chunk_tile(q, k, v, acc, den, old):
    s = scores_of(q, k)
    top = jnp.maximum(old, jnp.max(s, axis=1, keepdims=True))
    p = jnp.concatenate(
        [jnp.exp2((s[:, j:j + HEAD] - top) * SCALE) for j in range(0, s.shape[1], HEAD)], axis=1).astype(jnp.bfloat16)
    sums = jnp.dot(p, v, preferred_element_type=jnp.float32)
    keep = jnp.exp2((old - top) * SCALE)
    return acc * keep + sums[:, :HEAD], den * keep + sums[:, HEAD:], top


def cell(r, tile, head):
    rows = slice(r * tile, (r + 1) * tile)
    if isinstance(head, int):
        return rows, slice(head * HEAD, (head + 1) * HEAD)
    return rows, pl.ds(pl.multiple_of(head * HEAD, HEAD), HEAD)


def column(h, width=HEAD):
    return slice(h * width, (h + 1) * width) if isinstance(h, int) else pl.ds(pl.multiple_of(h * width, width), width)


def state_shapes(query):
    return [pltpu.VMEM(query.shape, jnp.float32)] * 3


def cost(rows, heads, blocks):
    work = rows * rows * heads * blocks
    return pl.CostEstimate(flops=4 * work * HEAD, transcendentals=work, bytes_accessed=rows * heads * HEAD * 16)


def add_chunk(q_ref, before, state, kv, h, group, tile):
    k, v = kv
    v = with_ones(v)
    for i in range(group):
        for r in range(q_ref.shape[0] // tile):
            at = cell(r, tile, h * group + i)
            new = chunk_tile(q_ref[at], k, v, before[0][at], before[1][at], before[2][at])
            for ref, value in zip(state, new):
                ref[at] = value


def own_and_local(me, sel, query, span_keys, span_values, keys, values, per_owner, group):
    rows, half = query.shape[0], query.shape[0] // 2
    kv_heads = span_keys.shape[1] // HEAD

    def body(me_ref, sel_ref, q_ref, sk_ref, sv_ref, k_ref, v_ref, *refs):
        state, mask_ref = refs[:3], refs[3]
        qpos = lax.broadcasted_iota(jnp.int32, (half, half), 0)
        kpos = lax.broadcasted_iota(jnp.int32, (half, half), 1)
        mask_ref[...] = jnp.where(kpos <= qpos, 0.0, NEG)

        def one_head(h, carry):
            col = column(h)
            own_k, own_v = sk_ref[:, col], with_ones(sv_ref[:, col])
            work = [(r, cell(r, half, h * group + i)) for r in range(2) for i in range(group)]
            queries = [q_ref[at] for _, at in work]

            def scores(j):
                return scores_of(queries[j], own_k[:(work[j][0] + 1) * half])

            done, s = [], scores(0)
            for j, (r, at) in enumerate(work):
                following = scores(j + 1) if j + 1 < len(work) else None
                done.append(own_rest(s, own_v[:(r + 1) * half], mask_ref[...], r * half))
                s = following
            for (_, at), new in zip(work, done):
                for ref, value in zip(state, new):
                    ref[at] = value
            if per_owner:
                @pl.when(wants(sel_ref, me_ref[0], h, per_owner))
                def _():
                    at = pl.ds(pl.multiple_of(local_row(sel_ref, me_ref[0], h, per_owner) * rows, rows), rows)
                    add_chunk(q_ref, state, state, (k_ref[at, col], v_ref[at, col]), h, group, rows // 4)
            return carry

        lax.fori_loop(0, kv_heads, one_head, 0)

    return pl.pallas_call(
        body, out_shape=state_shapes(query), in_specs=[SMEM] * 2 + [VMEM] * 5, out_specs=[VMEM] * 3,
        scratch_shapes=[pltpu.VMEM((half, half), jnp.float32)],
        compiler_params=WIDE, cost_estimate=cost(rows, kv_heads * group, 2),
    )(me, sel, *map(in_hbm, (query, span_keys, span_values, keys, values)))


def more_chunks(me, sel, query, sources, state, group, kv_heads, blocks):
    rows, half = query.shape[0], query.shape[0] // 2
    arrays = [a for s in sources for a in s[0]]

    def body(me_ref, sel_ref, q_ref, *refs):
        refs, old, state = refs[:len(arrays)], refs[len(arrays):len(arrays) + 3], refs[len(arrays) + 3:]
        def one_head(h, carry):
            cols = column(h, group * HEAD)
            at = 0
            for i, source in enumerate(sources):
                mine = refs[at:at + len(source[0])]
                at += len(source[0])
                needed = source[1](me_ref[0], sel_ref, h)

                @pl.when(needed)
                def _():
                    kv = source[2](mine, me_ref[0], sel_ref, h)
                    add_chunk(q_ref, state if i else old, state, kv, h, group, rows // 4)

                if i == 0:
                    @pl.when(jnp.logical_not(needed))
                    def _():
                        for new, previous in zip(state, old):
                            new[:, cols] = previous[:, cols]
            return carry

        lax.fori_loop(0, kv_heads, one_head, 0)

    n = 3 + len(arrays)
    return pl.pallas_call(
        body, out_shape=state_shapes(query), in_specs=[SMEM] * 2 + [VMEM] * (n + 1), out_specs=[VMEM] * 3,
        compiler_params=PARAMS, cost_estimate=cost(rows, kv_heads * group, blocks),
    )(me, sel, *map(near_core, (query, *arrays, *state)))


def finish(me, sel, query, arrays, when, read, state, group, head, out):
    rows = query.shape[0]
    tile = rows // 4
    first = head * group

    def body(me_ref, sel_ref, q_ref, *refs):
        refs, state, (o_ref, buf, sem) = refs[:len(arrays)], refs[len(arrays):len(arrays) + 3], refs[-3:]

        def tiles(fn):
            copies = []
            for i in range(group):
                for r in range(rows // tile):
                    acc, den = fn(cell(r, tile, first + i))
                    buf[cell(r, tile, i)] = (acc / den).astype(jnp.bfloat16)
                copies.append(pltpu.make_async_copy(
                    buf.at[:, pl.ds(i * HEAD, HEAD)], o_ref.at[:, pl.ds((first + i) * HEAD, HEAD)], sem.at[i]))
                copies[-1].start()
            for copy in copies:
                copy.wait()

        needed = when(me_ref[0], sel_ref, head)

        @pl.when(needed)
        def _():
            k, v = read(refs, me_ref[0], sel_ref, head)
            v = with_ones(v)
            tiles(lambda at: chunk_tile(q_ref[at], k, v, state[0][at], state[1][at], state[2][at])[:2])

        @pl.when(jnp.logical_not(needed))
        def _():
            tiles(lambda at: (state[0][at], state[1][at]))

    extra = [] if out is None else [out]
    n = 6 + len(arrays)
    return pl.pallas_call(
        body, out_shape=jax.ShapeDtypeStruct(query.shape, jnp.bfloat16),
        in_specs=[SMEM] * 2 + [VMEM] * (n - 2) + [ANY] * len(extra), out_specs=ANY,
        scratch_shapes=[pltpu.VMEM((rows, group * HEAD), jnp.bfloat16), pltpu.SemaphoreType.DMA((group,))],
        input_output_aliases={n: 0} if extra else {},
        compiler_params=PARAMS, cost_estimate=cost(rows, group, 1),
    )(me, sel, *map(near_core, (query, *arrays, *state)), *extra)


def pick(me, sels, arrays, rows, jobs, place=near_core):
    n, k = len(sels), len(arrays)

    def body(me_ref, *refs):
        sel_refs, refs, outs = refs[:n], refs[n:n + k], refs[n + k:]
        for out, parts in zip(outs, jobs):
            for when, keys, values, row, h, slot in parts:
                def copy():
                    at = pl.ds(pl.multiple_of(row(me_ref[0], sel_refs, h) * rows, rows), rows)
                    col = slice(h * HEAD, (h + 1) * HEAD)
                    out[2 * slot * rows:(2 * slot + 1) * rows] = refs[keys][at, col]
                    out[(2 * slot + 1) * rows:(2 * slot + 2) * rows] = refs[values][at, col]
                if when is None:
                    copy()
                else:
                    pl.when(when(me_ref[0]))(copy)

    shapes = [pltpu.VMEM((2 * rows * (1 + max(p[5] for p in parts)), HEAD), jnp.bfloat16) for parts in jobs]
    return pl.pallas_call(
        body, out_shape=shapes, in_specs=[SMEM] * (1 + n) + [VMEM] * k, out_specs=[VMEM] * len(jobs),
        compiler_params=PARAMS,
        cost_estimate=pl.CostEstimate(flops=0, transcendentals=0, bytes_accessed=8 * rows * HEAD * len(jobs)),
    )(me, *sels, *map(place, arrays))


def gathered(query, span_keys, span_values, cache_keys, stored_values, selected, group):
    rows = query.shape[0]
    kv_heads = span_keys.shape[1] // HEAD
    me = lax.axis_index("ctx").astype(jnp.int32).reshape(1)
    keys = lax.all_gather(cache_keys, "ctx", axis=0, tiled=True)
    values = lax.all_gather(stored_values, "ctx", axis=0, tiled=True)
    state = own_and_local(me, selected, query, span_keys, span_values, cache_keys, stored_values, 0, group)

    def always(m, s, h):
        return m >= 0

    def chosen(array, h, slot):
        start = jnp.clip(selected[0, h, slot], 0, keys.shape[0] // rows - 1) * rows
        return lax.dynamic_slice(array, (start, h * HEAD), (rows, HEAD))

    def stacked(refs, m, s, h):
        start = pl.multiple_of(2 * h * rows, rows)
        return refs[0][pl.ds(start, rows)], refs[0][pl.ds(start + rows, rows)]

    blocks = [[jnp.concatenate([chosen(a, h, slot) for h in range(kv_heads) for a in (keys, values)])] for slot in range(2)]
    state = more_chunks(me, selected, query, [(blocks[0], always, stacked)], state, group, kv_heads, 1)
    out = None
    for h in range(kv_heads):
        out = finish(me, selected, query, blocks[1], always, stacked, state, group, h, out)
    return out


def line_of_four(query, span_keys, span_values, cache_keys, stored_values, selected, group):
    rows = query.shape[0]
    kv_heads = span_keys.shape[1] // HEAD
    per_owner = cache_keys.shape[0] // rows
    me = lax.axis_index("ctx").astype(jnp.int32).reshape(1)
    heads = range(kv_heads)

    def inner(m):
        return (m == 1) | (m == 2)

    def outer(m):
        return (m == 0) | (m == 3)

    sel1 = lax.ppermute(selected, "ctx", [(0, 1), (1, 0), (2, 3), (3, 2)])
    mid_keys = lax.ppermute(cache_keys, "ctx", [(1, 2), (2, 1)])
    mid_values = lax.ppermute(stored_values, "ctx", [(1, 2), (2, 1)])
    both = lax.ppermute(jnp.concatenate([selected, sel1], axis=0), "ctx", [(3, 0), (0, 3)])

    out = pick(
        me, (sel1, both), (cache_keys, stored_values), rows,
        [[(None, 0, 1, lambda m, s, h: local_row(s[0], m, h, per_owner), h, 0)] for h in heads] +
        [[(outer, 0, 1, lambda m, s, h: local_row(s[1], m, h, per_owner), h, 0)] for h in heads], in_hbm)
    near_out, far_out = out[:kv_heads], out[kv_heads:]
    near = [lax.ppermute(n, "ctx", [(0, 1), (1, 0), (2, 3), (3, 2)]) for n in near_out]
    far = [lax.ppermute(f, "ctx", [(0, 3), (3, 0)]) for f in far_out[:-1]]

    near_out, far_out, span_keys = lax.optimization_barrier((near_out, far_out, span_keys))
    state = own_and_local(me, selected, query, span_keys, span_values, cache_keys, stored_values, per_owner, group)
    far_last, state = lax.optimization_barrier((far_out[-1], state))
    last = lax.ppermute(far_last, "ctx", [(0, 3), (3, 0)])
    far_last, state = lax.optimization_barrier((far_last, state))

    def single(refs, m, s, h):
        return refs[0][:rows], refs[0][rows:]

    near, far, state = lax.optimization_barrier((near, far, state))

    def stack(refs, m, s, h):
        k, v = refs[0][:rows], refs[0][rows:]
        for i in range(1, len(refs)):
            k, v = jnp.where(h == i, refs[i][:rows], k), jnp.where(h == i, refs[i][rows:], v)
        return k, v

    state = more_chunks(
        me, selected, query,
        [(tuple(near), lambda m, s, h: wants(s, m ^ 1, h, per_owner) & jnp.logical_not(wants(s, m, h, per_owner)), stack),
         (tuple(far), lambda m, s, h: outer(m) & (h < kv_heads - 1) & wants(s, m ^ 3, h, per_owner)
          & wants(s, m ^ 2, h, per_owner), stack)],
        state, group, kv_heads, 1)

    mid_keys, mid_values, state = lax.optimization_barrier((mid_keys, mid_values, state))
    cross_out = pick(
        me, (sel1, both), (cache_keys, stored_values, mid_keys, mid_values), rows,
        [[(inner, 2, 3, lambda m, s, h: local_row(s[0], m ^ 3, h, per_owner), h, 0),
          (outer, 0, 1, lambda m, s, h: local_row(s[1], m, h, per_owner, 1), h, 0)] for h in heads])
    cross = [lax.ppermute(c, "ctx", [(0, 2), (3, 1), (1, 0), (2, 3)]) for c in cross_out]

    def stacked(refs, m, s, h):
        start = pl.multiple_of(2 * h * rows, rows)
        return refs[0][pl.ds(start, rows)], refs[0][pl.ds(start + rows, rows)]

    def middle(refs, m, s, h):
        at = pl.ds(pl.multiple_of(local_row(s, m ^ 3, h, per_owner) * rows, rows), rows)
        return refs[0][at, column(h)], refs[1][at, column(h)]

    last, cross_out, state = lax.optimization_barrier((last, cross_out, state))
    state = more_chunks(
        me, selected, query,
        [((mid_keys, mid_values), lambda m, s, h: inner(m) & wants(s, m ^ 3, h, per_owner), middle),
         ((*far, last), lambda m, s, h: outer(m) & wants(s, m ^ 3, h, per_owner)
          & ((h == kv_heads - 1) | jnp.logical_not(wants(s, m ^ 2, h, per_owner))), stack),
         (tuple(near), lambda m, s, h: wants(s, m ^ 1, h, per_owner) & wants(s, m, h, per_owner), stack)],
        state, group, kv_heads, 1)
    out = None
    for h in heads:
        out = finish(me, selected, query, (cross[h],), lambda m, s, h: wants(s, m ^ 2, h, per_owner),
                     single, state, group, h, out)
    return out


def solution(mesh):
    kv = P(("groups", "ctx"), "mp")
    plan = line_of_four if mesh.shape["ctx"] == 4 else gathered

    def per_device(query, span_keys, span_values, cache_keys, stored_values, selected):
        group = query.shape[1] // span_keys.shape[1]
        return plan(query, span_keys, span_values, cache_keys, stored_values, selected, group)

    return jax.shard_map(
        per_device, mesh=mesh, in_specs=(kv, kv, kv, kv, kv, P(("groups", "ctx"), "mp", None)),
        out_specs=kv, check_vma=False)
```

profile of v0, /device:TPU:0, one launch (start us, length us, event | category | flops | bytes accessed | tf_op | source)
XLA Modules:
  0.0 60.7 jit_solution(15970083072706789136)
XLA Ops:
  0.0 3.0 %collective-permute-start = (s32[1,2,2]{2,1,0:T(2,128)}, s32[1,2,2]{2,1,0:T(2,128)S(1)}, u32[]{:S(2)}, u32[]{:S(2)}) collective-permute-start(s32[1,2,2]{2,1,0:T(2,128)} %sel_ref.9), channel_id=1, source_target_pairs={{0,4},{4,0},{8,12},{12,8},{1,5},{5,1},{9,13},{13,9},{2,6},{6,2},{1... | collective-permute-start | bytes 56 | tf_op jit(solution)/shard_map/ppermute | solution.py:286
  3.0 0.7 %collective-permute-start.2 = (bf16[1024,256]{1,0:T(8,128)(2,1)}, bf16[1024,256]{1,0:T(8,128)(2,1)S(1)}, u32[]{:S(2)}, u32[]{:S(2)}) collective-permute-start(bf16[1024,256]{1,0:T(8,128)(2,1)} %refs_2_.3), channel_id=1, source_target_pairs={{4,8},{8,4},{5,9},{9,5},{6,10},{10,6},{7,11},{11,7},{20,24},{24,20... | collective-permute-start | bytes 1572872 | tf_op jit(solution)/shard_map/ppermute | solution.py:287
  3.7 0.7 %collective-permute-start.3 = (bf16[1024,256]{1,0:T(8,128)(2,1)}, bf16[1024,256]{1,0:T(8,128)(2,1)S(1)}, u32[]{:S(2)}, u32[]{:S(2)}) collective-permute-start(bf16[1024,256]{1,0:T(8,128)(2,1)} %refs_3_.3), channel_id=1, source_target_pairs={{4,8},{8,4},{5,9},{9,5},{6,10},{10,6},{7,11},{11,7},{20,24},{24,20... | collective-permute-start | bytes 1572872 | tf_op jit(solution)/shard_map/ppermute | solution.py:288
  4.4 0.4 collective-permute-done.refs_0_
  4.8 0.7 %pad_add_fusion = s32[2,2,2]{2,1,0:T(2,128)S(1)} fusion(s32[1,2,2]{2,1,0:T(2,128)S(1)} %collective-permute-done.refs_0_, s32[1,2,2]{2,1,0:T(2,128)} %sel_ref.9), kind=kLoop, calls=%fused_computation | loop fusion | flops 8 | bytes 64 | tf_op jit(solution)/shard_map/concatenate | solution.py:289
  5.5 5.9 %collective-permute-start.1 = (s32[2,2,2]{2,1,0:T(2,128)S(1)}, s32[2,2,2]{2,1,0:T(2,128)S(1)}, u32[]{:S(2)}, u32[]{:S(2)}) collective-permute-start(s32[2,2,2]{2,1,0:T(2,128)S(1)} %pad_add_fusion), channel_id=1, source_target_pairs={{12,0},{0,12},{13,1},{1,13},{14,2},{2,14},{15,3},{3,15},{28,16},{1... | collective-permute-start | bytes 104 | tf_op jit(solution)/shard_map/ppermute | solution.py:289
  11.4 1.6 %collective-permute-done.1.refs_1_ = s32[2,2,2]{2,1,0:T(2,128)S(1)} collective-permute-done((s32[2,2,2]{2,1,0:T(2,128)S(1)}, s32[2,2,2]{2,1,0:T(2,128)S(1)}, u32[]{:S(2)}, u32[]{:S(2)}) %collective-permute-start.1) | collective-permute-done | bytes 64 | tf_op jit(solution)/shard_map/ppermute | solution.py:289
  13.1 1.4 %shard_map.64 = (bf16[1024,128]{1,0:T(8,128)(2,1)S(1)}, bf16[1024,128]{1,0:T(8,128)(2,1)S(1)}, bf16[1024,128]{1,0:T(8,128)(2,1)S(1)}, bf16[1024,128]{1,0:T(8,128)(2,1)S(1)}) custom-call(s32[1]{0:T(128)} %bitcast.me_ref, s32[1,2,2]{2,1,0:T(2,128)S(1)} %collective-permute-done.refs_0_, s32[2,2,2]{2,1,0:T(2,128)S(1)} %collective-permute-done.1.refs_1_, ...), custom_call_target="tpu_custom_call" | custom-call | bytes 2097152 | tf_op jit(solution)/shard_map/pallas_call | solution.py:239
  14.5 0.1 collective-permute-start.4
  14.6 2.0 %collective-permute-start.5 = (bf16[1024,128]{1,0:T(8,128)(2,1)S(1)}, bf16[1024,128]{1,0:T(8,128)(2,1)S(1)}, u32[]{:S(2)}, u32[]{:S(2)}) collective-permute-start(bf16[1024,128]{1,0:T(8,128)(2,1)S(1)} %get-tuple-element.48), channel_id=1, source_target_pairs={{0,4},{4,0},{8,12},{12,8},{1,5},{5,1},{9,13},{13,9},{2,6},{6,2},{1... | collective-permute-start | bytes 786440 | tf_op jit(solution)/shard_map/ppermute | solution.py:296
  16.6 5.7 %collective-permute-start.6 = (bf16[1024,128]{1,0:T(8,128)(2,1)S(1)}, bf16[1024,128]{1,0:T(8,128)(2,1)S(1)}, u32[]{:S(2)}, u32[]{:S(2)}) collective-permute-start(bf16[1024,128]{1,0:T(8,128)(2,1)S(1)} %get-tuple-element.49), channel_id=1, source_target_pairs={{0,12},{12,0},{1,13},{13,1},{2,14},{14,2},{3,15},{15,3},{16,28},{2... | collective-permute-start | bytes 786440 | tf_op jit(solution)/shard_map/ppermute | solution.py:297
  22.3 0.7 %copy-done.3 = s32[1,2,2]{2,1,0:T(2,128)S(1)} copy-done((s32[1,2,2]{2,1,0:T(2,128)S(1)}, s32[1,2,2]{2,1,0:T(2,128)}, u32[]{:S(2)}) %copy-start.3) | copy-done | bytes 40
  23.0 13.1 %shard_map.65 = (f32[512,2048]{1,0:T(8,128)S(1)}, f32[512,2048]{1,0:T(8,128)S(1)}, f32[512,2048]{1,0:T(8,128)S(1)}) custom-call(s32[1]{0:T(128)} %bitcast.me_ref, s32[1,2,2]{2,1,0:T(2,128)S(1)} %copy-done.3, bf16[512,2048]{1,0:T(8,128)(2,1)} %q_ref.9, bf16[512,256]{1,0:T(8,128)(2,1)} %sk_ref, bf16[512,256]{1,0:T(8,128)(2,1)} %sv_ref.1, ...), custom_call_target="tpu_custom_call" | custom-call | flops 4294967296 | bytes 16777216 | tf_op jit(solution)/shard_map/pallas_call | solution.py:136
  36.1 2.1 %collective-permute-start.8 = (bf16[1024,128]{1,0:T(8,128)(2,1)S(1)}, bf16[1024,128]{1,0:T(8,128)(2,1)S(1)}, u32[]{:S(2)}, u32[]{:S(2)}) collective-permute-start(bf16[1024,128]{1,0:T(8,128)(2,1)S(1)} %get-tuple-element.74), channel_id=1, source_target_pairs={{0,12},{12,0},{1,13},{13,1},{2,14},{14,2},{3,15},{15,3},{16,28},{2... | collective-permute-start | bytes 786440 | tf_op jit(solution)/shard_map/ppermute | solution.py:302
  38.3 0.0 copy-start.1
  38.3 1.4 %shard_map.66 = (f32[512,2048]{1,0:T(8,128)S(1)}, f32[512,2048]{1,0:T(8,128)S(1)}, f32[512,2048]{1,0:T(8,128)S(1)}) custom-call(s32[1]{0:T(128)} %bitcast.me_ref, s32[1,2,2]{2,1,0:T(2,128)S(1)} %copy-done.3, bf16[512,2048]{1,0:T(8,128)(2,1)S(1)} %copy-done, bf16[1024,128]{1,0:T(8,128)(2,1)S(1)} %collective-permute-done.4.refs_0_.refs_4_, ...), custom_call_target="tpu_custom_call" | custom-call | flops 2147483648 | bytes 16777216 | tf_op jit(solution)/shard_map/pallas_call | solution.py:172
  39.8 0.7 %shard_map.67 = (bf16[1024,128]{1,0:T(8,128)(2,1)S(1)}, bf16[1024,128]{1,0:T(8,128)(2,1)S(1)}) custom-call(s32[1]{0:T(128)} %bitcast.me_ref, s32[1,2,2]{2,1,0:T(2,128)S(1)} %collective-permute-done.refs_0_, s32[2,2,2]{2,1,0:T(2,128)S(1)} %collective-permute-done.1.refs_1_, bf16[1024,256]{1,0:T(8,128)(2,1)S(1)} %copy-done.1, bf16[1024,256]{1,0:T(8,128)(2,1)S(1)} %copy-done.2, ...), custom_call_target="tpu_custom_call" | custom-call | bytes 1048576 | tf_op jit(solution)/shard_map/pallas_call | solution.py:239
  40.5 1.1 %collective-permute-start.9 = (bf16[1024,128]{1,0:T(8,128)(2,1)S(1)}, bf16[1024,128]{1,0:T(8,128)(2,1)S(1)}, u32[]{:S(2)}, u32[]{:S(2)}) collective-permute-start(bf16[1024,128]{1,0:T(8,128)(2,1)S(1)} %get-tuple-element.75), channel_id=1, source_target_pairs={{0,8},{12,4},{4,0},{8,12},{1,9},{13,5},{5,1},{9,13},{2,10},{14,6},... | collective-permute-start | bytes 786440 | tf_op jit(solution)/shard_map/ppermute | solution.py:328
  41.6 6.6 %collective-permute-start.7 = (bf16[1024,128]{1,0:T(8,128)(2,1)S(1)}, bf16[1024,128]{1,0:T(8,128)(2,1)S(1)}, u32[]{:S(2)}, u32[]{:S(2)}) collective-permute-start(bf16[1024,128]{1,0:T(8,128)(2,1)S(1)} %get-tuple-element.73), channel_id=1, source_target_pairs={{0,8},{12,4},{4,0},{8,12},{1,9},{13,5},{5,1},{9,13},{2,10},{14,6},... | collective-permute-start | bytes 786440 | tf_op jit(solution)/shard_map/ppermute | solution.py:328
  48.1 0.9 %collective-permute-done.8.refs_3_ = bf16[1024,128]{1,0:T(8,128)(2,1)S(1)} collective-permute-done((bf16[1024,128]{1,0:T(8,128)(2,1)S(1)}, bf16[1024,128]{1,0:T(8,128)(2,1)S(1)}, u32[]{:S(2)}, u32[]{:S(2)}) %collective-permute-start.8) | collective-permute-done | bytes 262176 | tf_op jit(solution)/shard_map/ppermute | solution.py:302
  49.0 4.5 %shard_map.68 = (f32[512,2048]{1,0:T(8,128)S(1)}, f32[512,2048]{1,0:T(8,128)S(1)}, f32[512,2048]{1,0:T(8,128)S(1)}) custom-call(s32[1]{0:T(128)} %bitcast.me_ref, s32[1,2,2]{2,1,0:T(2,128)S(1)} %copy-done.3, bf16[512,2048]{1,0:T(8,128)(2,1)S(1)} %copy-done, bf16[1024,256]{1,0:T(8,128)(2,1)S(1)} %collective-permute-done.2.refs_4_.refs_0_, ...), custom_call_target="tpu_custom_call" | custom-call | flops 2147483648 | bytes 16777216 | tf_op jit(solution)/shard_map/pallas_call | solution.py:172
  53.6 2.0 %shard_map.69.refs_4_ = bf16[512,2048]{1,0:T(8,128)(2,1)} custom-call(s32[1]{0:T(128)} %bitcast.me_ref, s32[1,2,2]{2,1,0:T(2,128)S(1)} %copy-done.3, bf16[512,2048]{1,0:T(8,128)(2,1)S(1)} %copy-done, bf16[1024,128]{1,0:T(8,128)(2,1)S(1)} %collective-permute-done.9.refs_0_, f32[512,2048]{1,0:T(8,128)S(1)} %get-tuple-element.83.refs_1_, ...), custom_call_target="tpu_custom_call" | custom-call | flops 1073741824 | bytes 8388608 | tf_op jit(solution)/shard_map/pallas_call | solution.py:212
  55.6 0.4 collective-permute-done.7.refs_0_
  56.0 4.5 %shard_map.70 = bf16[512,2048]{1,0:T(8,128)(2,1)} custom-call(s32[1]{0:T(128)} %bitcast.me_ref, s32[1,2,2]{2,1,0:T(2,128)S(1)} %copy-done.3, bf16[512,2048]{1,0:T(8,128)(2,1)S(1)} %copy-done, bf16[1024,128]{1,0:T(8,128)(2,1)S(1)} %collective-permute-done.7.refs_0_, f32[512,2048]{1,0:T(8,128)S(1)} %get-tuple-element.83.refs_1_, ...), custom_call_target="tpu_custom_call", output_to_operand_aliasing={{}: (7, {})} | custom-call | flops 1073741824 | bytes 8388608 | tf_op jit(solution)/shard_map/pallas_call | solution.py:212
  (12 shorter events, 0.0 us)
Async XLA Ops:
  0.0 4.8 %collective-permute-start = (s32[1,2,2]{2,1,0:T(2,128)}, s32[1,2,2]{2,1,0:T(2,128)S(1)}, u32[]{:S(2)}, u32[]{:S(2)}) collective-permute-start(s32[1,2,2]{2,1,0:T(2,128)} %sel_ref.9), channel_id=1, source_target_pairs={{0,4},{4,0},{8,12},{12,8},{1,5},{5,1},{9,13},{13,9},{2,6},{6,2},{1... | collective-permute-start | bytes 56 | tf_op jit(solution)/shard_map/ppermute | solution.py:286
  3.0 36.7 %collective-permute-start.2 = (bf16[1024,256]{1,0:T(8,128)(2,1)}, bf16[1024,256]{1,0:T(8,128)(2,1)S(1)}, u32[]{:S(2)}, u32[]{:S(2)}) collective-permute-start(bf16[1024,256]{1,0:T(8,128)(2,1)} %refs_2_.3), channel_id=1, source_target_pairs={{4,8},{8,4},{5,9},{9,5},{6,10},{10,6},{7,11},{11,7},{20,24},{24,20... | collective-permute-start | bytes 1572872 | tf_op jit(solution)/shard_map/ppermute | solution.py:287
  3.7 36.1 %collective-permute-start.3 = (bf16[1024,256]{1,0:T(8,128)(2,1)}, bf16[1024,256]{1,0:T(8,128)(2,1)S(1)}, u32[]{:S(2)}, u32[]{:S(2)}) collective-permute-start(bf16[1024,256]{1,0:T(8,128)(2,1)} %refs_3_.3), channel_id=1, source_target_pairs={{4,8},{8,4},{5,9},{9,5},{6,10},{10,6},{7,11},{11,7},{20,24},{24,20... | collective-permute-start | bytes 1572872 | tf_op jit(solution)/shard_map/ppermute | solution.py:288
  5.5 7.6 %collective-permute-start.1 = (s32[2,2,2]{2,1,0:T(2,128)S(1)}, s32[2,2,2]{2,1,0:T(2,128)S(1)}, u32[]{:S(2)}, u32[]{:S(2)}) collective-permute-start(s32[2,2,2]{2,1,0:T(2,128)S(1)} %pad_add_fusion), channel_id=1, source_target_pairs={{12,0},{0,12},{13,1},{1,13},{14,2},{2,14},{15,3},{3,15},{28,16},{1... | collective-permute-start | bytes 104 | tf_op jit(solution)/shard_map/ppermute | solution.py:289
  14.5 21.6 %collective-permute-start.4 = (bf16[1024,128]{1,0:T(8,128)(2,1)S(1)}, bf16[1024,128]{1,0:T(8,128)(2,1)S(1)}, u32[]{:S(2)}, u32[]{:S(2)}) collective-permute-start(bf16[1024,128]{1,0:T(8,128)(2,1)S(1)} %get-tuple-element.47), channel_id=1, source_target_pairs={{0,4},{4,0},{8,12},{12,8},{1,5},{5,1},{9,13},{13,9},{2,6},{6,2},{1... | collective-permute-start | bytes 786440 | tf_op jit(solution)/shard_map/ppermute | solution.py:296
  14.6 23.7 %collective-permute-start.5 = (bf16[1024,128]{1,0:T(8,128)(2,1)S(1)}, bf16[1024,128]{1,0:T(8,128)(2,1)S(1)}, u32[]{:S(2)}, u32[]{:S(2)}) collective-permute-start(bf16[1024,128]{1,0:T(8,128)(2,1)S(1)} %get-tuple-element.48), channel_id=1, source_target_pairs={{0,4},{4,0},{8,12},{12,8},{1,5},{5,1},{9,13},{13,9},{2,6},{6,2},{1... | collective-permute-start | bytes 786440 | tf_op jit(solution)/shard_map/ppermute | solution.py:296
  16.6 21.7 %collective-permute-start.6 = (bf16[1024,128]{1,0:T(8,128)(2,1)S(1)}, bf16[1024,128]{1,0:T(8,128)(2,1)S(1)}, u32[]{:S(2)}, u32[]{:S(2)}) collective-permute-start(bf16[1024,128]{1,0:T(8,128)(2,1)S(1)} %get-tuple-element.49), channel_id=1, source_target_pairs={{0,12},{12,0},{1,13},{13,1},{2,14},{14,2},{3,15},{15,3},{16,28},{2... | collective-permute-start | bytes 786440 | tf_op jit(solution)/shard_map/ppermute | solution.py:297
  22.3 0.7 %copy-start.3 = (s32[1,2,2]{2,1,0:T(2,128)S(1)}, s32[1,2,2]{2,1,0:T(2,128)}, u32[]{:S(2)}) copy-start(s32[1,2,2]{2,1,0:T(2,128)} %sel_ref.9) | copy-start | bytes 52
  23.0 15.3 %copy-start = (bf16[512,2048]{1,0:T(8,128)(2,1)S(1)}, bf16[512,2048]{1,0:T(8,128)(2,1)}, u32[]{:S(2)}) copy-start(bf16[512,2048]{1,0:T(8,128)(2,1)} %q_ref.9) | copy-start | bytes 6291460
  36.1 12.9 %collective-permute-start.8 = (bf16[1024,128]{1,0:T(8,128)(2,1)S(1)}, bf16[1024,128]{1,0:T(8,128)(2,1)S(1)}, u32[]{:S(2)}, u32[]{:S(2)}) collective-permute-start(bf16[1024,128]{1,0:T(8,128)(2,1)S(1)} %get-tuple-element.74), channel_id=1, source_target_pairs={{0,12},{12,0},{1,13},{13,1},{2,14},{14,2},{3,15},{15,3},{16,28},{2... | collective-permute-start | bytes 786440 | tf_op jit(solution)/shard_map/ppermute | solution.py:302
  38.3 1.5 %copy-start.1 = (bf16[1024,256]{1,0:T(8,128)(2,1)S(1)}, bf16[1024,256]{1,0:T(8,128)(2,1)}, u32[]{:S(2)}) copy-start(bf16[1024,256]{1,0:T(8,128)(2,1)} %refs_2_.3) | copy-start | bytes 1572868
  38.3 1.5 %copy-start.2 = (bf16[1024,256]{1,0:T(8,128)(2,1)S(1)}, bf16[1024,256]{1,0:T(8,128)(2,1)}, u32[]{:S(2)}) copy-start(bf16[1024,256]{1,0:T(8,128)(2,1)} %refs_3_.3) | copy-start | bytes 1572868
  40.5 13.1 %collective-permute-start.9 = (bf16[1024,128]{1,0:T(8,128)(2,1)S(1)}, bf16[1024,128]{1,0:T(8,128)(2,1)S(1)}, u32[]{:S(2)}, u32[]{:S(2)}) collective-permute-start(bf16[1024,128]{1,0:T(8,128)(2,1)S(1)} %get-tuple-element.75), channel_id=1, source_target_pairs={{0,8},{12,4},{4,0},{8,12},{1,9},{13,5},{5,1},{9,13},{2,10},{14,6},... | collective-permute-start | bytes 786440 | tf_op jit(solution)/shard_map/ppermute | solution.py:328
  41.6 14.4 %collective-permute-start.7 = (bf16[1024,128]{1,0:T(8,128)(2,1)S(1)}, bf16[1024,128]{1,0:T(8,128)(2,1)S(1)}, u32[]{:S(2)}, u32[]{:S(2)}) collective-permute-start(bf16[1024,128]{1,0:T(8,128)(2,1)S(1)} %get-tuple-element.73), channel_id=1, source_target_pairs={{0,8},{12,4},{4,0},{8,12},{1,9},{13,5},{5,1},{9,13},{2,10},{14,6},... | collective-permute-start | bytes 786440 | tf_op jit(solution)/shard_map/ppermute | solution.py:328
where the time goes:
time: 61.8 us; the launch traced here: 60.7 us
  starting transfers between devices  27.9 us (45%)
  Pallas kernels  27.8 us (45%)
  waiting for transfers between devices  3.28 us (5%)
  local copies, waits for them, and re-layouts  0.69 us (1%)
  other arithmetic  0.68 us (1%)
    pallas_call x1, Pallas kernels, own_and_local(): pl.pallas_call(body, out_shape=state_shapes(query), in_specs=[SMEM] * 2 +...  13.1 us
    ppermute x2, starting transfers between devices, line_of_four(): lax.ppermute(c, 'ctx', [(0, 2), (3, 1), (1, 0), (2, 3)])  7.62 us
    pallas_call x2, Pallas kernels, finish(): pl.pallas_call(body, out_shape=jax.ShapeDtypeStruct(query.shape, jnp.bflo...  6.52 us
    pallas_call x2, Pallas kernels, more_chunks(): pl.pallas_call(body, out_shape=state_shapes(query), in_specs=[SMEM] * 2 +...  5.98 us
    ppermute x1, starting transfers between devices, line_of_four(): lax.ppermute(jnp.concatenate([selected, sel1], axis=0), 'ctx', [(3, 0), (...  5.94 us
    ppermute x1, starting transfers between devices, line_of_four(): far = [lax.ppermute(f, 'ctx', [(0, 3), (3, 0)]) for f in far_out[:-1]]  5.71 us
    ppermute x1, starting transfers between devices, line_of_four(): sel1 = lax.ppermute(selected, 'ctx', [(0, 1), (1, 0), (2, 3), (3, 2)])  3.02 us
    pallas_call x2, Pallas kernels, pick(): pl.pallas_call(body, out_shape=shapes, in_specs=[SMEM] * (1 + n) + [VMEM]...  2.14 us
  transfers between devices with their start and end apart: 10, of which 4 were waited for; matrix products, arithmetic and copies ran while one was open for 1% of the time, Pallas kernels for 38%

commit v1 on v0

--- a/solution.py
+++ b/solution.py
@@ -175,24 +175,34 @@
     )(me, sel, *map(near_core, (query, *arrays, *state)))
 
 
-def finish(me, sel, query, arrays, when, read, state, group, head, out):
+def finish(me, sel, query, arrays, when, read, state, group, head, parts):
     rows = query.shape[0]
     tile = rows // 4
     first = head * group
+    width = group * HEAD
+    whole = len(parts) == query.shape[1] // width - 1
 
     def body(me_ref, sel_ref, q_ref, *refs):
-        refs, state, (o_ref, buf, sem) = refs[:len(arrays)], refs[len(arrays):len(arrays) + 3], refs[-3:]
+        part_refs = refs[len(arrays) + 3:len(arrays) + 3 + len(parts)] if whole else ()
+        refs, state, rest = refs[:len(arrays)], refs[len(arrays):len(arrays) + 3], refs[len(arrays) + 3 + len(part_refs):]
+        o_ref = rest[0]
+        buf = rest[1] if whole else o_ref
+        copies = [pltpu.make_async_copy(part, o_ref.at[:, pl.ds(i * width, width)], rest[2].at[group + i])
+                  for i, part in enumerate(part_refs)]
+        for copy in copies:
+            copy.start()
 
         def tiles(fn):
-            copies = []
+            own = []
             for i in range(group):
                 for r in range(rows // tile):
                     acc, den = fn(cell(r, tile, first + i))
                     buf[cell(r, tile, i)] = (acc / den).astype(jnp.bfloat16)
-                copies.append(pltpu.make_async_copy(
-                    buf.at[:, pl.ds(i * HEAD, HEAD)], o_ref.at[:, pl.ds((first + i) * HEAD, HEAD)], sem.at[i]))
-                copies[-1].start()
-            for copy in copies:
+                if whole:
+                    own.append(pltpu.make_async_copy(
+                        buf.at[:, pl.ds(i * HEAD, HEAD)], o_ref.at[:, pl.ds((first + i) * HEAD, HEAD)], rest[2].at[i]))
+                    own[-1].start()
+            for copy in own:
                 copy.wait()
 
         needed = when(me_ref[0], sel_ref, head)
@@ -207,15 +217,17 @@
         def _():
             tiles(lambda at: (state[0][at], state[1][at]))
 
-    extra = [] if out is None else [out]
-    n = 6 + len(arrays)
+        for copy in copies:
+            copy.wait()
+
+    n = 4 + len(arrays) + (len(parts) if whole else 0)
+    scratch = [pltpu.VMEM((rows, width), jnp.bfloat16), pltpu.SemaphoreType.DMA((group + len(parts),))]
     return pl.pallas_call(
-        body, out_shape=jax.ShapeDtypeStruct(query.shape, jnp.bfloat16),
-        in_specs=[SMEM] * 2 + [VMEM] * (n - 2) + [ANY] * len(extra), out_specs=ANY,
-        scratch_shapes=[pltpu.VMEM((rows, group * HEAD), jnp.bfloat16), pltpu.SemaphoreType.DMA((group,))],
-        input_output_aliases={n: 0} if extra else {},
+        body,
+        out_shape=jax.ShapeDtypeStruct(query.shape, jnp.bfloat16) if whole else pltpu.VMEM((rows, width), jnp.bfloat16),
+        in_specs=[SMEM] * 2 + [VMEM] * n, out_specs=ANY if whole else VMEM, scratch_shapes=scratch if whole else [],
         compiler_params=PARAMS, cost_estimate=cost(rows, group, 1),
-    )(me, sel, *map(near_core, (query, *arrays, *state)), *extra)
+    )(me, sel, *map(near_core, (query, *arrays, *state, *(parts if whole else ()))))
 
 
 def pick(me, sels, arrays, rows, jobs, place=near_core):
@@ -264,10 +276,10 @@
 
     blocks = [[jnp.concatenate([chosen(a, h, slot) for h in range(kv_heads) for a in (keys, values)])] for slot in range(2)]
     state = more_chunks(me, selected, query, [(blocks[0], always, stacked)], state, group, kv_heads, 1)
-    out = None
+    parts = []
     for h in range(kv_heads):
-        out = finish(me, selected, query, blocks[1], always, stacked, state, group, h, out)
-    return out
+        parts.append(finish(me, selected, query, blocks[1], always, stacked, state, group, h, parts))
+    return parts[-1]
 
 
 def line_of_four(query, span_keys, span_values, cache_keys, stored_values, selected, group):
@@ -343,11 +355,11 @@
           & ((h == kv_heads - 1) | jnp.logical_not(wants(s, m ^ 2, h, per_owner))), stack),
          (tuple(near), lambda m, s, h: wants(s, m ^ 1, h, per_owner) & wants(s, m, h, per_owner), stack)],
         state, group, kv_heads, 1)
-    out = None
+    parts = []
     for h in heads:
-        out = finish(me, selected, query, (cross[h],), lambda m, s, h: wants(s, m ^ 2, h, per_owner),
-                     single, state, group, h, out)
-    return out
+        parts.append(finish(me, selected, query, (cross[h],), lambda m, s, h: wants(s, m ^ 2, h, per_owner),
+                            single, state, group, h, parts))
+    return parts[-1]
 
 
 def solution(mesh):

time: 61.8 us -> 60.7 us (0.982)
    pallas_call x2, Pallas kernels: 6.52 us -> 3.23 us  [finish(): pl.pallas_call(body, out_shape=jax.ShapeDtypeStruct(query.shape, jnp.bflo...]
    pallas_call x2, Pallas kernels: 5.98 us -> 9.02 us  [more_chunks(): pl.pallas_call(body, out_shape=state_shapes(query), in_specs=[SMEM] * 2 +...]
  transfers between devices with their start and end apart: 10 -> 10, of which waited for: 4 -> 3; matrix products, arithmetic and copies ran while one was open for 1% -> 1% of each run, Pallas kernels for 38% -> 43%
where the time goes in v1:
time: 60.7 us; the launch traced here: 60.2 us
  starting transfers between devices  27.9 us (46%)
  Pallas kernels  27.5 us (45%)
  waiting for transfers between devices  3 us (5%)
  local copies, waits for them, and re-layouts  0.69 us (1%)
  other arithmetic  0.68 us (1%)
    pallas_call x1, Pallas kernels, own_and_local(): pl.pallas_call(body, out_shape=state_shapes(query), in_specs=[SMEM] * 2 +...  13.1 us
    pallas_call x2, Pallas kernels, more_chunks(): pl.pallas_call(body, out_shape=state_shapes(query), in_specs=[SMEM] * 2 +...  9.02 us
    ppermute x2, starting transfers between devices, line_of_four(): lax.ppermute(c, 'ctx', [(0, 2), (3, 1), (1, 0), (2, 3)])  7.61 us
    ppermute x1, starting transfers between devices, line_of_four(): lax.ppermute(jnp.concatenate([selected, sel1], axis=0), 'ctx', [(3, 0), (...  5.94 us
    ppermute x1, starting transfers between devices, line_of_four(): far = [lax.ppermute(f, 'ctx', [(0, 3), (3, 0)]) for f in far_out[:-1]]  5.71 us
    pallas_call x2, Pallas kernels, finish(): pl.pallas_call(body, out_shape=jax.ShapeDtypeStruct(query.shape, jnp.bflo...  3.23 us
    ppermute x1, starting transfers between devices, line_of_four(): sel1 = lax.ppermute(selected, 'ctx', [(0, 1), (1, 0), (2, 3), (3, 2)])  3.02 us
    pallas_call x2, Pallas kernels, pick(): pl.pallas_call(body, out_shape=shapes, in_specs=[SMEM] * (1 + n) + [VMEM]...  2.14 us
  transfers between devices with their start and end apart: 10, of which 3 were waited for; matrix products, arithmetic and copies ran while one was open for 1% of the time, Pallas kernels for 43%

profile of v1, /device:TPU:0, one launch (start us, length us, event | category | flops | bytes accessed | tf_op | source)
XLA Modules:
  0.0 60.2 jit_solution(4246849863518216498)
XLA Ops:
  0.0 3.0 %collective-permute-start = (s32[1,2,2]{2,1,0:T(2,128)}, s32[1,2,2]{2,1,0:T(2,128)S(1)}, u32[]{:S(2)}, u32[]{:S(2)}) collective-permute-start(s32[1,2,2]{2,1,0:T(2,128)} %sel_ref.9), channel_id=1, source_target_pairs={{0,4},{4,0},{8,12},{12,8},{1,5},{5,1},{9,13},{13,9},{2,6},{6,2},{1... | collective-permute-start | bytes 56 | tf_op jit(solution)/shard_map/ppermute | solution.py:298
  3.0 0.7 %collective-permute-start.2 = (bf16[1024,256]{1,0:T(8,128)(2,1)}, bf16[1024,256]{1,0:T(8,128)(2,1)S(1)}, u32[]{:S(2)}, u32[]{:S(2)}) collective-permute-start(bf16[1024,256]{1,0:T(8,128)(2,1)} %refs_2_.3), channel_id=1, source_target_pairs={{4,8},{8,4},{5,9},{9,5},{6,10},{10,6},{7,11},{11,7},{20,24},{24,20... | collective-permute-start | bytes 1572872 | tf_op jit(solution)/shard_map/ppermute | solution.py:299
  3.7 0.7 %collective-permute-start.3 = (bf16[1024,256]{1,0:T(8,128)(2,1)}, bf16[1024,256]{1,0:T(8,128)(2,1)S(1)}, u32[]{:S(2)}, u32[]{:S(2)}) collective-permute-start(bf16[1024,256]{1,0:T(8,128)(2,1)} %refs_3_.3), channel_id=1, source_target_pairs={{4,8},{8,4},{5,9},{9,5},{6,10},{10,6},{7,11},{11,7},{20,24},{24,20... | collective-permute-start | bytes 1572872 | tf_op jit(solution)/shard_map/ppermute | solution.py:300
  4.4 0.4 collective-permute-done.refs_0_
  4.8 0.7 %pad_add_fusion = s32[2,2,2]{2,1,0:T(2,128)S(1)} fusion(s32[1,2,2]{2,1,0:T(2,128)S(1)} %collective-permute-done.refs_0_, s32[1,2,2]{2,1,0:T(2,128)} %sel_ref.9), kind=kLoop, calls=%fused_computation | loop fusion | flops 8 | bytes 64 | tf_op jit(solution)/shard_map/concatenate | solution.py:301
  5.5 5.9 %collective-permute-start.1 = (s32[2,2,2]{2,1,0:T(2,128)S(1)}, s32[2,2,2]{2,1,0:T(2,128)S(1)}, u32[]{:S(2)}, u32[]{:S(2)}) collective-permute-start(s32[2,2,2]{2,1,0:T(2,128)S(1)} %pad_add_fusion), channel_id=1, source_target_pairs={{12,0},{0,12},{13,1},{1,13},{14,2},{2,14},{15,3},{3,15},{28,16},{1... | collective-permute-start | bytes 104 | tf_op jit(solution)/shard_map/ppermute | solution.py:301
  11.4 1.6 %collective-permute-done.1.refs_1_ = s32[2,2,2]{2,1,0:T(2,128)S(1)} collective-permute-done((s32[2,2,2]{2,1,0:T(2,128)S(1)}, s32[2,2,2]{2,1,0:T(2,128)S(1)}, u32[]{:S(2)}, u32[]{:S(2)}) %collective-permute-start.1) | collective-permute-done | bytes 64 | tf_op jit(solution)/shard_map/ppermute | solution.py:301
  13.1 1.4 %shard_map.64 = (bf16[1024,128]{1,0:T(8,128)(2,1)S(1)}, bf16[1024,128]{1,0:T(8,128)(2,1)S(1)}, bf16[1024,128]{1,0:T(8,128)(2,1)S(1)}, bf16[1024,128]{1,0:T(8,128)(2,1)S(1)}) custom-call(s32[1]{0:T(128)} %bitcast.me_ref, s32[1,2,2]{2,1,0:T(2,128)S(1)} %collective-permute-done.refs_0_, s32[2,2,2]{2,1,0:T(2,128)S(1)} %collective-permute-done.1.refs_1_, ...), custom_call_target="tpu_custom_call" | custom-call | bytes 2097152 | tf_op jit(solution)/shard_map/pallas_call | solution.py:251
  14.5 0.1 collective-permute-start.4
  14.6 2.0 %collective-permute-start.5 = (bf16[1024,128]{1,0:T(8,128)(2,1)S(1)}, bf16[1024,128]{1,0:T(8,128)(2,1)S(1)}, u32[]{:S(2)}, u32[]{:S(2)}) collective-permute-start(bf16[1024,128]{1,0:T(8,128)(2,1)S(1)} %get-tuple-element.48), channel_id=1, source_target_pairs={{0,4},{4,0},{8,12},{12,8},{1,5},{5,1},{9,13},{13,9},{2,6},{6,2},{1... | collective-permute-start | bytes 786440 | tf_op jit(solution)/shard_map/ppermute | solution.py:308
  16.6 5.7 %collective-permute-start.6 = (bf16[1024,128]{1,0:T(8,128)(2,1)S(1)}, bf16[1024,128]{1,0:T(8,128)(2,1)S(1)}, u32[]{:S(2)}, u32[]{:S(2)}) collective-permute-start(bf16[1024,128]{1,0:T(8,128)(2,1)S(1)} %get-tuple-element.49), channel_id=1, source_target_pairs={{0,12},{12,0},{1,13},{13,1},{2,14},{14,2},{3,15},{15,3},{16,28},{2... | collective-permute-start | bytes 786440 | tf_op jit(solution)/shard_map/ppermute | solution.py:309
  22.3 0.0 copy-start.3
  22.3 0.7 %copy-done.3 = s32[1,2,2]{2,1,0:T(2,128)S(1)} copy-done((s32[1,2,2]{2,1,0:T(2,128)S(1)}, s32[1,2,2]{2,1,0:T(2,128)}, u32[]{:S(2)}) %copy-start.3) | copy-done | bytes 40
  23.0 13.1 %shard_map.65 = (f32[512,2048]{1,0:T(8,128)S(1)}, f32[512,2048]{1,0:T(8,128)S(1)}, f32[512,2048]{1,0:T(8,128)S(1)}) custom-call(s32[1]{0:T(128)} %bitcast.me_ref, s32[1,2,2]{2,1,0:T(2,128)S(1)} %copy-done.3, bf16[512,2048]{1,0:T(8,128)(2,1)} %q_ref.9, bf16[512,256]{1,0:T(8,128)(2,1)} %sk_ref, bf16[512,256]{1,0:T(8,128)(2,1)} %sv_ref.1, ...), custom_call_target="tpu_custom_call" | custom-call | flops 4294967296 | bytes 16777216 | tf_op jit(solution)/shard_map/pallas_call | solution.py:136
  36.1 2.1 %collective-permute-start.8 = (bf16[1024,128]{1,0:T(8,128)(2,1)S(1)}, bf16[1024,128]{1,0:T(8,128)(2,1)S(1)}, u32[]{:S(2)}, u32[]{:S(2)}) collective-permute-start(bf16[1024,128]{1,0:T(8,128)(2,1)S(1)} %get-tuple-element.74), channel_id=1, source_target_pairs={{0,12},{12,0},{1,13},{13,1},{2,14},{14,2},{3,15},{15,3},{16,28},{2... | collective-permute-start | bytes 786440 | tf_op jit(solution)/shard_map/ppermute | solution.py:314
  38.3 0.0 copy-start.2
  38.3 1.4 %shard_map.66 = (f32[512,2048]{1,0:T(8,128)S(1)}, f32[512,2048]{1,0:T(8,128)S(1)}, f32[512,2048]{1,0:T(8,128)S(1)}) custom-call(s32[1]{0:T(128)} %bitcast.me_ref, s32[1,2,2]{2,1,0:T(2,128)S(1)} %copy-done.3, bf16[512,2048]{1,0:T(8,128)(2,1)S(1)} %copy-done, bf16[1024,128]{1,0:T(8,128)(2,1)S(1)} %collective-permute-done.4.refs_0_.refs_4_, ...), custom_call_target="tpu_custom_call" | custom-call | flops 2147483648 | bytes 16777216 | tf_op jit(solution)/shard_map/pallas_call | solution.py:172
  39.8 0.7 %shard_map.67 = (bf16[1024,128]{1,0:T(8,128)(2,1)S(1)}, bf16[1024,128]{1,0:T(8,128)(2,1)S(1)}) custom-call(s32[1]{0:T(128)} %bitcast.me_ref, s32[1,2,2]{2,1,0:T(2,128)S(1)} %collective-permute-done.refs_0_, s32[2,2,2]{2,1,0:T(2,128)S(1)} %collective-permute-done.1.refs_1_, bf16[1024,256]{1,0:T(8,128)(2,1)S(1)} %copy-done.1, bf16[1024,256]{1,0:T(8,128)(2,1)S(1)} %copy-done.2, ...), custom_call_target="tpu_custom_call" | custom-call | bytes 1048576 | tf_op jit(solution)/shard_map/pallas_call | solution.py:251
  40.5 0.1 collective-permute-start.9
  40.6 7.6 %collective-permute-start.7 = (bf16[1024,128]{1,0:T(8,128)(2,1)S(1)}, bf16[1024,128]{1,0:T(8,128)(2,1)S(1)}, u32[]{:S(2)}, u32[]{:S(2)}) collective-permute-start(bf16[1024,128]{1,0:T(8,128)(2,1)S(1)} %get-tuple-element.73), channel_id=1, source_target_pairs={{0,8},{12,4},{4,0},{8,12},{1,9},{13,5},{5,1},{9,13},{2,10},{14,6},... | collective-permute-start | bytes 786440 | tf_op jit(solution)/shard_map/ppermute | solution.py:340
  48.1 1.0 %collective-permute-done.8.refs_3_ = bf16[1024,128]{1,0:T(8,128)(2,1)S(1)} collective-permute-done((bf16[1024,128]{1,0:T(8,128)(2,1)S(1)}, bf16[1024,128]{1,0:T(8,128)(2,1)S(1)}, u32[]{:S(2)}, u32[]{:S(2)}) %collective-permute-start.8) | collective-permute-done | bytes 262176 | tf_op jit(solution)/shard_map/ppermute | solution.py:314
  49.1 7.6 %shard_map.68 = (f32[512,2048]{1,0:T(8,128)S(1)}, f32[512,2048]{1,0:T(8,128)S(1)}, f32[512,2048]{1,0:T(8,128)S(1)}) custom-call(s32[1]{0:T(128)} %bitcast.me_ref, s32[1,2,2]{2,1,0:T(2,128)S(1)} %copy-done.3, bf16[512,2048]{1,0:T(8,128)(2,1)S(1)} %copy-done, bf16[1024,256]{1,0:T(8,128)(2,1)S(1)} %collective-permute-done.2.refs_4_.refs_0_, ...), custom_call_target="tpu_custom_call" | custom-call | flops 2147483648 | bytes 16777216 | tf_op jit(solution)/shard_map/pallas_call | solution.py:172
  56.7 1.3 %shard_map.69.refs_4_ = bf16[512,1024]{1,0:T(8,128)(2,1)S(1)} custom-call(s32[1]{0:T(128)} %bitcast.me_ref, s32[1,2,2]{2,1,0:T(2,128)S(1)} %copy-done.3, bf16[512,2048]{1,0:T(8,128)(2,1)S(1)} %copy-done, bf16[1024,128]{1,0:T(8,128)(2,1)S(1)} %collective-permute-done.9.refs_0_, f32[512,2048]{1,0:T(8,128)S(1)} %get-tuple-element.83.refs_1_, ...), custom_call_target="tpu_custom_call" | custom-call | flops 1073741824 | bytes 8388608 | tf_op jit(solution)/shard_map/pallas_call | solution.py:225
  58.0 1.9 %shard_map.70 = bf16[512,2048]{1,0:T(8,128)(2,1)} custom-call(s32[1]{0:T(128)} %bitcast.me_ref, s32[1,2,2]{2,1,0:T(2,128)S(1)} %copy-done.3, bf16[512,2048]{1,0:T(8,128)(2,1)S(1)} %copy-done, bf16[1024,128]{1,0:T(8,128)(2,1)S(1)} %collective-permute-done.7.refs_0_, f32[512,2048]{1,0:T(8,128)S(1)} %get-tuple-element.83.refs_1_, ...), custom_call_target="tpu_custom_call" | custom-call | flops 1073741824 | bytes 8388608 | tf_op jit(solution)/shard_map/pallas_call | solution.py:225
  (12 shorter events, 0.0 us)
Async XLA Ops:
  0.0 4.8 %collective-permute-start = (s32[1,2,2]{2,1,0:T(2,128)}, s32[1,2,2]{2,1,0:T(2,128)S(1)}, u32[]{:S(2)}, u32[]{:S(2)}) collective-permute-start(s32[1,2,2]{2,1,0:T(2,128)} %sel_ref.9), channel_id=1, source_target_pairs={{0,4},{4,0},{8,12},{12,8},{1,5},{5,1},{9,13},{13,9},{2,6},{6,2},{1... | collective-permute-start | bytes 56 | tf_op jit(solution)/shard_map/ppermute | solution.py:298
  3.0 36.7 %collective-permute-start.2 = (bf16[1024,256]{1,0:T(8,128)(2,1)}, bf16[1024,256]{1,0:T(8,128)(2,1)S(1)}, u32[]{:S(2)}, u32[]{:S(2)}) collective-permute-start(bf16[1024,256]{1,0:T(8,128)(2,1)} %refs_2_.3), channel_id=1, source_target_pairs={{4,8},{8,4},{5,9},{9,5},{6,10},{10,6},{7,11},{11,7},{20,24},{24,20... | collective-permute-start | bytes 1572872 | tf_op jit(solution)/shard_map/ppermute | solution.py:299
  3.7 36.1 %collective-permute-start.3 = (bf16[1024,256]{1,0:T(8,128)(2,1)}, bf16[1024,256]{1,0:T(8,128)(2,1)S(1)}, u32[]{:S(2)}, u32[]{:S(2)}) collective-permute-start(bf16[1024,256]{1,0:T(8,128)(2,1)} %refs_3_.3), channel_id=1, source_target_pairs={{4,8},{8,4},{5,9},{9,5},{6,10},{10,6},{7,11},{11,7},{20,24},{24,20... | collective-permute-start | bytes 1572872 | tf_op jit(solution)/shard_map/ppermute | solution.py:300
  5.5 7.6 %collective-permute-start.1 = (s32[2,2,2]{2,1,0:T(2,128)S(1)}, s32[2,2,2]{2,1,0:T(2,128)S(1)}, u32[]{:S(2)}, u32[]{:S(2)}) collective-permute-start(s32[2,2,2]{2,1,0:T(2,128)S(1)} %pad_add_fusion), channel_id=1, source_target_pairs={{12,0},{0,12},{13,1},{1,13},{14,2},{2,14},{15,3},{3,15},{28,16},{1... | collective-permute-start | bytes 104 | tf_op jit(solution)/shard_map/ppermute | solution.py:301
  14.5 21.6 %collective-permute-start.4 = (bf16[1024,128]{1,0:T(8,128)(2,1)S(1)}, bf16[1024,128]{1,0:T(8,128)(2,1)S(1)}, u32[]{:S(2)}, u32[]{:S(2)}) collective-permute-start(bf16[1024,128]{1,0:T(8,128)(2,1)S(1)} %get-tuple-element.47), channel_id=1, source_target_pairs={{0,4},{4,0},{8,12},{12,8},{1,5},{5,1},{9,13},{13,9},{2,6},{6,2},{1... | collective-permute-start | bytes 786440 | tf_op jit(solution)/shard_map/ppermute | solution.py:308
  14.6 23.7 %collective-permute-start.5 = (bf16[1024,128]{1,0:T(8,128)(2,1)S(1)}, bf16[1024,128]{1,0:T(8,128)(2,1)S(1)}, u32[]{:S(2)}, u32[]{:S(2)}) collective-permute-start(bf16[1024,128]{1,0:T(8,128)(2,1)S(1)} %get-tuple-element.48), channel_id=1, source_target_pairs={{0,4},{4,0},{8,12},{12,8},{1,5},{5,1},{9,13},{13,9},{2,6},{6,2},{1... | collective-permute-start | bytes 786440 | tf_op jit(solution)/shard_map/ppermute | solution.py:308
  16.6 21.7 %collective-permute-start.6 = (bf16[1024,128]{1,0:T(8,128)(2,1)S(1)}, bf16[1024,128]{1,0:T(8,128)(2,1)S(1)}, u32[]{:S(2)}, u32[]{:S(2)}) collective-permute-start(bf16[1024,128]{1,0:T(8,128)(2,1)S(1)} %get-tuple-element.49), channel_id=1, source_target_pairs={{0,12},{12,0},{1,13},{13,1},{2,14},{14,2},{3,15},{15,3},{16,28},{2... | collective-permute-start | bytes 786440 | tf_op jit(solution)/shard_map/ppermute | solution.py:309
  22.3 0.7 %copy-start.3 = (s32[1,2,2]{2,1,0:T(2,128)S(1)}, s32[1,2,2]{2,1,0:T(2,128)}, u32[]{:S(2)}) copy-start(s32[1,2,2]{2,1,0:T(2,128)} %sel_ref.9) | copy-start | bytes 52
  23.0 15.3 %copy-start = (bf16[512,2048]{1,0:T(8,128)(2,1)S(1)}, bf16[512,2048]{1,0:T(8,128)(2,1)}, u32[]{:S(2)}) copy-start(bf16[512,2048]{1,0:T(8,128)(2,1)} %q_ref.9) | copy-start | bytes 6291460
  36.1 13.0 %collective-permute-start.8 = (bf16[1024,128]{1,0:T(8,128)(2,1)S(1)}, bf16[1024,128]{1,0:T(8,128)(2,1)S(1)}, u32[]{:S(2)}, u32[]{:S(2)}) collective-permute-start(bf16[1024,128]{1,0:T(8,128)(2,1)S(1)} %get-tuple-element.74), channel_id=1, source_target_pairs={{0,12},{12,0},{1,13},{13,1},{2,14},{14,2},{3,15},{15,3},{16,28},{2... | collective-permute-start | bytes 786440 | tf_op jit(solution)/shard_map/ppermute | solution.py:314
  38.3 1.5 %copy-start.1 = (bf16[1024,256]{1,0:T(8,128)(2,1)S(1)}, bf16[1024,256]{1,0:T(8,128)(2,1)}, u32[]{:S(2)}) copy-start(bf16[1024,256]{1,0:T(8,128)(2,1)} %refs_2_.3) | copy-start | bytes 1572868
  38.3 1.5 %copy-start.2 = (bf16[1024,256]{1,0:T(8,128)(2,1)S(1)}, bf16[1024,256]{1,0:T(8,128)(2,1)}, u32[]{:S(2)}) copy-start(bf16[1024,256]{1,0:T(8,128)(2,1)} %refs_3_.3) | copy-start | bytes 1572868
  40.5 16.2 %collective-permute-start.9 = (bf16[1024,128]{1,0:T(8,128)(2,1)S(1)}, bf16[1024,128]{1,0:T(8,128)(2,1)S(1)}, u32[]{:S(2)}, u32[]{:S(2)}) collective-permute-start(bf16[1024,128]{1,0:T(8,128)(2,1)S(1)} %get-tuple-element.75), channel_id=1, source_target_pairs={{0,8},{12,4},{4,0},{8,12},{1,9},{13,5},{5,1},{9,13},{2,10},{14,6},... | collective-permute-start | bytes 786440 | tf_op jit(solution)/shard_map/ppermute | solution.py:340
  40.6 17.4 %collective-permute-start.7 = (bf16[1024,128]{1,0:T(8,128)(2,1)S(1)}, bf16[1024,128]{1,0:T(8,128)(2,1)S(1)}, u32[]{:S(2)}, u32[]{:S(2)}) collective-permute-start(bf16[1024,128]{1,0:T(8,128)(2,1)S(1)} %get-tuple-element.73), channel_id=1, source_target_pairs={{0,8},{12,4},{4,0},{8,12},{1,9},{13,5},{5,1},{9,13},{2,10},{14,6},... | collective-permute-start | bytes 786440 | tf_op jit(solution)/shard_map/ppermute | solution.py:340
